TPU v7x, 512 devices: a whole 4x4x16 slice. The times are simulated.
512 devices in a mesh: dp: 4 (over y), expert: 32 (over z, core), tensor: 4 (over x).
Axes of the slice: x: 4, y: 4, z: 16, core: 2. Of those that a mesh axis runs over, the one named last changes fastest.
Arguments:
- tokens: bfloat16 [16384, 2048], P(('dp', 'expert')), may hold values from -6 to 6
- cotangent: bfloat16 [16384, 2048], P(('dp', 'expert')), may hold values from -6 to 6
- expert_ids: int32 [16384, 1], P(('dp', 'expert')), may hold values from 0 to 31; in each aligned block of 128 rows (0 to 127, 128 to 255, ...) at most 8 rows name the same one
- gate_weight: bfloat16 [32, 2048, 1408], P('expert', 'dp', 'tensor'), may hold values from -0.125 to 0.125
- up_weight: bfloat16 [32, 2048, 1408], P('expert', 'dp', 'tensor'), may hold values from -0.125 to 0.125
- down_weight: bfloat16 [32, 2048, 1408], P('expert', 'dp', 'tensor'), may hold values from -0.15625 to 0.15625
Outputs:
- grad_tokens: bfloat16 [16384, 2048], P(('dp', 'expert'), 'tensor')
- grad_gate: bfloat16 [32, 2048, 1408], P('expert', 'dp', 'tensor')
- grad_up: bfloat16 [32, 2048, 1408], P('expert', 'dp', 'tensor')
Inputs may be any that keep to these rules, and one draw needn't show every extreme that they name: `expert_ids`: among the 128 tokens of one block no expert id occurs more than 8 times, and in every draw some block holds some id exactly 8 times.
All inputs are finite; a program needn't handle non-finite values.
Results may differ from a plain program's by a relative error of at most 0.013.
Values may be sent and summed in bfloat16 or wider, within the bound.
A program may use at most 64 MiB of HBM per device.

v0:
```python
import jax
import jax.numpy as jnp
from jax import lax
from jax.sharding import PartitionSpec as P

CAP = 8


def bucket_matrix(expert_ids, expert_count, capacity):
    chosen = expert_ids[:, 0]
    columns = jnp.arange(expert_count, dtype=jnp.int32)
    onehot = (chosen[:, None] == columns[None, :]).astype(jnp.int32)
    earlier = jnp.cumsum(onehot, axis=0) - onehot
    position = jnp.sum(earlier * onehot, axis=1)
    target = chosen * capacity + position
    slot_rows = jnp.arange(expert_count * capacity, dtype=jnp.int32)
    return (slot_rows[:, None] == target[None, :]).astype(jnp.bfloat16)


def on_device(tokens, cotangent, expert_ids, gate_weight, up_weight, down_weight):
    owners = lax.axis_size("expert")
    feature_count = tokens.shape[1]
    local_experts = gate_weight.shape[0]
    expert_count = local_experts * owners
    slot_count = owners * CAP
    placer = bucket_matrix(expert_ids, expert_count, CAP)
    gate_full, up_full, down_full = (
        lax.all_gather(gate_weight, "dp", axis=1, tiled=True),
        lax.all_gather(up_weight, "dp", axis=1, tiled=True),
        lax.all_gather(down_weight, "dp", axis=1, tiled=True),
    )

    def to_buckets(rows):
        packed = jnp.dot(placer, rows, preferred_element_type=jnp.float32).astype(jnp.bfloat16)
        return packed.reshape(owners, local_experts, CAP, rows.shape[1])

    arrived_tokens, arrived_grads = (
        lax.all_to_all(to_buckets(tokens), "expert", split_axis=0, concat_axis=2, tiled=True),
        lax.all_to_all(to_buckets(cotangent), "expert", split_axis=0, concat_axis=2, tiled=True),
    )
    inputs = arrived_tokens.reshape(local_experts, slot_count, feature_count)
    grads_in = arrived_grads.reshape(local_experts, slot_count, feature_count)
    gate_act = jnp.einsum("esd,edf->esf", inputs, gate_full, preferred_element_type=jnp.float32)
    up_act = jnp.einsum("esd,edf->esf", inputs, up_full, preferred_element_type=jnp.float32)
    hidden_grad = jnp.einsum(
        "esd,edf->esf", grads_in, down_full, preferred_element_type=jnp.float32
    )
    sigmoid_gate = jax.nn.sigmoid(gate_act)
    up_grad = (hidden_grad * gate_act * sigmoid_gate).astype(jnp.bfloat16)
    gate_grad = (
        hidden_grad * up_act * sigmoid_gate * (1.0 + gate_act * (1.0 - sigmoid_gate))
    ).astype(jnp.bfloat16)
    partial_value = jnp.einsum(
        "esf,edf->esd", gate_grad, gate_full, preferred_element_type=jnp.float32
    )
    partial_value = partial_value + jnp.einsum(
        "esf,edf->esd", up_grad, up_full, preferred_element_type=jnp.float32
    )
    gate_term = jnp.einsum("esd,esf->edf", inputs, gate_grad, preferred_element_type=jnp.float32)
    up_term = jnp.einsum("esd,esf->edf", inputs, up_grad, preferred_element_type=jnp.float32)
    grad_gate, grad_up = (
        lax.psum_scatter(
            gate_term.astype(jnp.bfloat16), "dp", scatter_dimension=1, tiled=True
        ).astype(jnp.float32),
        lax.psum_scatter(
            up_term.astype(jnp.bfloat16), "dp", scatter_dimension=1, tiled=True
        ).astype(jnp.float32),
    )
    contract = (((0,), (0,)), ((), ()))
    outgoing_back = partial_value.astype(jnp.bfloat16).reshape(
        1, local_experts, slot_count, feature_count
    )
    returned = lax.all_to_all(outgoing_back, "expert", split_axis=2, concat_axis=0, tiled=True)
    flat_rows = returned.reshape(expert_count * CAP, feature_count)
    per_token = lax.dot_general(placer, flat_rows, contract, preferred_element_type=jnp.float32)
    summed = lax.psum_scatter(
        per_token.astype(jnp.bfloat16), "tensor", scatter_dimension=1, tiled=True
    )
    return (summed, grad_gate.astype(jnp.bfloat16), grad_up.astype(jnp.bfloat16))


def solution(mesh):
    placed = (
        P(("dp", "expert"), None),
        P(("dp", "expert"), None),
        P(("dp", "expert"), None),
        P("expert", "dp", "tensor"),
        P("expert", "dp", "tensor"),
        P("expert", "dp", "tensor"),
    )
    return jax.shard_map(
        on_device,
        mesh=mesh,
        in_specs=placed,
        out_specs=(
            P(("dp", "expert"), "tensor"),
            P("expert", "dp", "tensor"),
            P("expert", "dp", "tensor"),
        ),
        check_vma=False,
    )
```

profile of v0, /device:TPU:8, one launch (start us, length us, event | category | flops | bytes accessed | tf_op | source)
XLA Modules:
  0.0 280.9 jit_solution(13116984333326666507)
XLA Ops:
  7.2 0.8 fusion.37
  8.2 0.8 select_reduce_fusion
  9.7 1.4 fusion.5
  11.1 15.6 %all-to-all-start.1 = ((bf16[32,1,8,2048]{3,2,1,0:T(8,128)(2,1)}), bf16[32,1,8,2048]{3,2,1,0:T(8,128)(2,1)S(1)}, u32[]{:S(2)}, u32[]{:S(2)}) async-start(bf16[32,1,8,2048]{3,2,1,0:T(8,128)(2,1)} %fusion.5), calls=%async_computation.1 | async-start | bytes 2097152 | tf_op jit(solution)/shard_map/all_to_all | solution.py:38
  27.4 1.4 fusion.4
  28.8 53.8 %all-to-all-done.1 = bf16[32,1,8,2048]{3,2,1,0:T(8,128)(2,1)S(1)} async-done(((bf16[32,1,8,2048]{3,2,1,0:T(8,128)(2,1)}), bf16[32,1,8,2048]{3,2,1,0:T(8,128)(2,1)S(1)}, u32[]{:S(2)}, u32[]{:S(2)}) %all-to-all-start.1) | async-done | bytes 1048608 | tf_op jit(solution)/shard_map/all_to_all | solution.py:38
  82.7 3.9 %all-to-all-start = ((bf16[32,1,8,2048]{3,2,1,0:T(8,128)(2,1)}), bf16[32,1,8,2048]{3,2,1,0:T(8,128)(2,1)S(1)}, u32[]{:S(2)}, u32[]{:S(2)}) async-start(bf16[32,1,8,2048]{3,2,1,0:T(8,128)(2,1)} %fusion.4), calls=%async_computation | async-start | bytes 2097152 | tf_op jit(solution)/shard_map/all_to_all | solution.py:39
  88.3 1.9 fusion.8
  90.3 32.8 %all-gather.4.cloned.1.call-done = bf16[1,2048,352]{1,2,0:T(8,128)(2,1)} async-done(((bf16[1,512,352]{1,2,0:T(8,128)(2,1)}), bf16[1,2048,352]{1,2,0:T(8,128)(2,1)}) %all-gather.4.cloned.1.call-update) | async-done | bytes 1441808 | tf_op jit(solution)/shard_map/all_gather | solution.py:30
  123.0 20.1 %all-to-all-done = bf16[32,1,8,2048]{3,2,1,0:T(8,128)(2,1)S(1)} async-done(((bf16[32,1,8,2048]{3,2,1,0:T(8,128)(2,1)}), bf16[32,1,8,2048]{3,2,1,0:T(8,128)(2,1)S(1)}, u32[]{:S(2)}, u32[]{:S(2)}) %all-to-all-start) | async-done | bytes 1048608 | tf_op jit(solution)/shard_map/all_to_all | solution.py:39
  143.1 2.7 multiply_convert_fusion
  145.9 13.1 %all-gather.6.cloned.1.call-done = bf16[1,2048,352]{1,2,0:T(8,128)(2,1)} async-done(((bf16[1,512,352]{1,2,0:T(8,128)(2,1)}), bf16[1,2048,352]{1,2,0:T(8,128)(2,1)}) %all-gather.6.cloned.1.call-update) | async-done | bytes 1441808 | tf_op jit(solution)/shard_map/all_gather | solution.py:29
  158.9 2.0 fusion.24
  160.9 1.7 fusion.1
  164.0 0.7 fusion.3
  164.7 2.9 %copy.21 = bf16[1,1,256,2048]{3,1,0,2:T(2,128)(2,1)} copy(bf16[1,1,256,2048]{3,2,1,0:T(8,128)(2,1)S(1)} %fusion.3) | data formatting | bytes 2097152 | tf_op jit(solution)/shard_map/reshape | solution.py:70
  168.2 8.0 %reduce = bf16[256,2048]{1,0:T(8,128)(2,1)S(1)} reduce(bf16[256,1,1,2048]{3,2,1,0:T(2,128)(2,1)} %bitcast.66, bf16[]{:T(256)} %broadcast.19), dimensions={1,2}, to_apply=%bitcast.65.reduce_sub_computation | reduce | bytes 2097154
  176.2 1.9 reshape.108
  178.1 12.6 %all-to-all-start.2 = ((bf16[32,2,8192]{2,1,0:T(2,128)(2,1)}), bf16[32,2,8192]{2,1,0:T(2,128)(2,1)S(1)}, u32[]{:S(2)}, u32[]{:S(2)}) async-start(bf16[32,2,8192]{2,1,0:T(2,128)(2,1)} %reshape.108), calls=%async_computation.2 | async-start | bytes 2097152 | tf_op jit(solution)/shard_map/all_to_all | solution.py:73
  190.8 1.7 fusion.2
  192.5 54.2 %all-to-all-done.2 = bf16[32,2,8192]{2,1,0:T(2,128)(2,1)S(1)} async-done(((bf16[32,2,8192]{2,1,0:T(2,128)(2,1)}), bf16[32,2,8192]{2,1,0:T(2,128)(2,1)S(1)}, u32[]{:S(2)}, u32[]{:S(2)}) %all-to-all-start.2) | async-done | bytes 1048608 | tf_op jit(solution)/shard_map/all_to_all | solution.py:73
  246.7 3.5 %reshape.109 = bf16[256,1,1,2048]{3,2,1,0:T(2,128)(2,1)} reshape(bf16[32,2,8192]{2,1,0:T(2,128)(2,1)S(1)} %all-to-all-done.2) | data formatting | bytes 2097152
  250.1 3.1 %convolution_convert_fusion.4 = bf16[128,2048]{1,0:T(8,128)(2,1)} fusion(bf16[1,1,256,2048]{3,1,0,2:T(2,128)(2,1)} %bitcast.67, s32[128]{0:T(128)S(1)} %multiply_add_fusion), kind=kOutput, calls=%fused_computation.11 | convolution fusion | flops 134512640 | bytes 1573376 | tf_op jit(solution)/shard_map/dot_general | solution.py:75
  253.4 20.7 %reduce-scatter.4.cloned.1.call-done = bf16[128,512]{1,0:T(8,128)(2,1)} async-done(((bf16[128,2048]{1,0:T(8,128)(2,1)}), bf16[128,512]{1,0:T(8,128)(2,1)}) %reduce-scatter.4.cloned.1.call-update) | async-done | bytes 131088 | tf_op jit(solution)/shard_map/reduce_scatter | solution.py:76
  (27 shorter events, 5.3 us)
Async XLA Ops:
  7.2 2.5 copy-start
  11.1 16.4 %copy-start.3 = (bf16[128,2048]{1,0:T(8,128)(2,1)S(1)}, bf16[128,2048]{1,0:T(8,128)(2,1)}, u32[]{:S(2)}) copy-start(bf16[128,2048]{1,0:T(8,128)(2,1)} %param.7) | copy-start | bytes 1572868
  11.1 71.6 %all-to-all-start.1 = ((bf16[32,1,8,2048]{3,2,1,0:T(8,128)(2,1)}), bf16[32,1,8,2048]{3,2,1,0:T(8,128)(2,1)S(1)}, u32[]{:S(2)}, u32[]{:S(2)}) async-start(bf16[32,1,8,2048]{3,2,1,0:T(8,128)(2,1)} %fusion.5), calls=%async_computation.1 | async-start | bytes 2097152 | tf_op jit(solution)/shard_map/all_to_all | solution.py:38
  26.7 61.7 %all-gather.8.cloned.1.call-start = ((), (), s32[]{:S(2)}) async-start(), calls=%async_computation.8 | async-start | bytes 1802240 | tf_op jit(solution)/shard_map/all_gather | solution.py:28
  82.7 60.4 %all-to-all-start = ((bf16[32,1,8,2048]{3,2,1,0:T(8,128)(2,1)}), bf16[32,1,8,2048]{3,2,1,0:T(8,128)(2,1)S(1)}, u32[]{:S(2)}, u32[]{:S(2)}) async-start(bf16[32,1,8,2048]{3,2,1,0:T(8,128)(2,1)} %fusion.4), calls=%async_computation | async-start | bytes 2097152 | tf_op jit(solution)/shard_map/all_to_all | solution.py:39
  86.6 36.4 %all-gather.4.cloned.1.call-start = ((), (), s32[]{:S(2)}) async-start(), calls=%async_computation.6 | async-start | bytes 1802240 | tf_op jit(solution)/shard_map/all_gather | solution.py:30
  87.4 71.6 %all-gather.6.cloned.1.call-start = ((), (), s32[]{:S(2)}) async-start(), calls=%async_computation.7 | async-start | bytes 1802240 | tf_op jit(solution)/shard_map/all_gather | solution.py:29
  88.1 165.2 %reduce-scatter.6.cloned.1.call-start = ((), (), s32[]{:S(2)}) async-start(), calls=%async_computation.10 | async-start | bytes 1802240 | tf_op jit(solution)/shard_map/reduce_scatter | solution.py:62
  160.9 1.7 copy-start.1
  162.6 1.4 copy-start.2
  178.1 68.6 %all-to-all-start.2 = ((bf16[32,2,8192]{2,1,0:T(2,128)(2,1)}), bf16[32,2,8192]{2,1,0:T(2,128)(2,1)S(1)}, u32[]{:S(2)}, u32[]{:S(2)}) async-start(bf16[32,2,8192]{2,1,0:T(2,128)(2,1)} %reshape.108), calls=%async_computation.2 | async-start | bytes 2097152 | tf_op jit(solution)/shard_map/all_to_all | solution.py:73
  190.7 62.6 %reduce-scatter.8.cloned.1.call-start = ((), (), s32[]{:S(2)}) async-start(), calls=%async_computation.11 | async-start | bytes 1802240 | tf_op jit(solution)/shard_map/reduce_scatter | solution.py:65
  192.4 81.7 %reduce-scatter.4.cloned.1.call-start = ((), (), s32[]{:S(2)}) async-start(), calls=%async_computation.9 | async-start | bytes 655360 | tf_op jit(solution)/shard_map/reduce_scatter | solution.py:76
Sparse Core Ops, SparseCore 0:
  29.6 33.4 all-gather.7
  89.5 33.4 all-gather.3
  125.1 33.7 all-gather.5
  162.8 32.7 reduce-scatter.5
  198.8 32.4 reduce-scatter.7
  253.4 20.6 reduce-scatter.3
where the time goes:
time: 282 us; the launch traced here: 281 us
  waiting for transfers between devices  197 us (70%)
  starting transfers between devices  32.5 us (12%)
  matrix products  17.4 us (6%)
  between operations  14.2 us (5%)
  other arithmetic  10.5 us (4%)
  local copies, waits for them, and re-layouts  9.44 us (3%)
    all_to_all x1, waiting for transfers between devices, on_device(): lax.all_to_all(outgoing_back, 'expert', split_axis=2, concat_axis=0, tile...  54.2 us
    all_to_all x1, waiting for transfers between devices, on_device(): lax.all_to_all(to_buckets(tokens), 'expert', split_axis=0, concat_axis=2,...  53.8 us
    all_gather x1, waiting for transfers between devices, on_device(): lax.all_gather(down_weight, 'dp', axis=1, tiled=True)  32.8 us
    reduce_scatter x1, waiting for transfers between devices, on_device(): lax.psum_scatter(per_token.astype(jnp.bfloat16), 'tensor', scatter_dimens...  20.7 us
    all_to_all x1, waiting for transfers between devices, on_device(): lax.all_to_all(to_buckets(cotangent), 'expert', split_axis=0, concat_axis...  20.1 us
    all_to_all x1, starting transfers between devices, on_device(): lax.all_to_all(to_buckets(tokens), 'expert', split_axis=0, concat_axis=2,...  15.6 us
    all_gather x1, waiting for transfers between devices, on_device(): lax.all_gather(up_weight, 'dp', axis=1, tiled=True)  13.1 us
    all_to_all x1, starting transfers between devices, on_device(): lax.all_to_all(outgoing_back, 'expert', split_axis=2, concat_axis=0, tile...  12.6 us
  transfers between devices with their start and end apart: 9, of which 6 were waited for; matrix products, arithmetic and copies ran while one was open for 10% of the time, Pallas kernels for 0%

commit v1 on v0

--- a/solution.py
+++ b/solution.py
@@ -24,10 +24,24 @@
     expert_count = local_experts * owners
     slot_count = owners * CAP
     placer = bucket_matrix(expert_ids, expert_count, CAP)
+
+    def serve_table_here(own_rows):
+        full_n = lax.axis_size("dp")
+        frames = tuple(((hop_no, (hop_no + 1) % full_n) for hop_no in range(full_n)))
+        shelf = tuple(((hop_no, (hop_no - 1) % full_n) for hop_no in range(full_n)))
+        out_arr, near = ([own_rows], [own_rows])
+        for _ in range(full_n // 2):
+            out_arr.append(lax.ppermute(out_arr[-1], axis_name="dp", perm=frames))
+        for _ in range((full_n - 1) // 2):
+            near.append(lax.ppermute(near[-1], axis_name="dp", perm=shelf))
+        wide_out = jnp.concatenate([*out_arr[::-1], *near[1:]], 1)
+        m_next = jnp.roll(wide_out, (lax.axis_index("dp") - full_n // 2) * own_rows.shape[1], 1)
+        return m_next
+
     gate_full, up_full, down_full = (
         lax.all_gather(gate_weight, "dp", axis=1, tiled=True),
         lax.all_gather(up_weight, "dp", axis=1, tiled=True),
-        lax.all_gather(down_weight, "dp", axis=1, tiled=True),
+        serve_table_here(down_weight),
     )
 
     def to_buckets(rows):

time: 282 us -> 286 us (1.014)
  waiting for transfers between devices: 197 us -> 186 us
  starting transfers between devices: 32.5 us -> 42.4 us
  local copies, waits for them, and re-layouts: 9.44 us -> 16 us
    all_gather x1 -> x0, waiting for transfers between devices: 32.8 us -> none  [on_device(): lax.all_gather(down_weight, 'dp', axis=1, tiled=True)]
    ppermute x0 -> x3, waiting for transfers between devices: none -> 20.6 us  [the longest x2 17 us: serve_table_here(): out_arr.append(lax.ppermute(out_arr[-1], axis_name='dp', perm=frames))]
    ppermute x0 -> x3, starting transfers between devices: none -> 9.5 us  [the longest x2 6.96 us: serve_table_here(): out_arr.append(lax.ppermute(out_arr[-1], axis_name='dp', perm=frames))]
    unnamed x11 -> x20, local copies, waits for them, and re-layouts: 6.51 us -> 12.2 us
    all_to_all x1, waiting for transfers between devices: 20.1 us -> 14.5 us  [on_device(): lax.all_to_all(to_buckets(cotangent), 'expert', split_axis=0, concat_axis...]
    all_gather x1, waiting for transfers between devices: 13.1 us -> 17.8 us  [on_device(): lax.all_gather(up_weight, 'dp', axis=1, tiled=True)]
  transfers between devices with their start and end apart: 9 -> 11, of which waited for: 6 -> 9; matrix products, arithmetic and copies ran while one was open for 10% -> 12% of each run, Pallas kernels for 0% -> 0%
where the time goes in v1:
time: 286 us; the launch traced here: 285 us
  waiting for transfers between devices  186 us (65%)
  starting transfers between devices  42.4 us (15%)
  matrix products  16.9 us (6%)
  local copies, waits for them, and re-layouts  16 us (6%)
  between operations  14 us (5%)
  other arithmetic  10.5 us (4%)
    all_to_all x1, waiting for transfers between devices, on_device(): lax.all_to_all(to_buckets(tokens), 'expert', split_axis=0, concat_axis=2,...  54.5 us
    all_to_all x1, waiting for transfers between devices, on_device(): lax.all_to_all(outgoing_back, 'expert', split_axis=2, concat_axis=0, tile...  54.2 us
    reduce_scatter x1, waiting for transfers between devices, on_device(): lax.psum_scatter(per_token.astype(jnp.bfloat16), 'tensor', scatter_dimens...  20.8 us
    all_gather x1, waiting for transfers between devices, on_device(): lax.all_gather(up_weight, 'dp', axis=1, tiled=True)  17.8 us
    ppermute x2, waiting for transfers between devices, serve_table_here(): out_arr.append(lax.ppermute(out_arr[-1], axis_name='dp', perm=frames))  17 us
    all_to_all x1, starting transfers between devices, on_device(): lax.all_to_all(to_buckets(tokens), 'expert', split_axis=0, concat_axis=2,...  15.5 us
    all_to_all x1, waiting for transfers between devices, on_device(): lax.all_to_all(to_buckets(cotangent), 'expert', split_axis=0, concat_axis...  14.5 us
    all_to_all x1, starting transfers between devices, on_device(): lax.all_to_all(outgoing_back, 'expert', split_axis=2, concat_axis=0, tile...  12.6 us
  transfers between devices with their start and end apart: 11, of which 9 were waited for; matrix products, arithmetic and copies ran while one was open for 12% of the time, Pallas kernels for 0%

profile of v1, /device:TPU:8, one launch (start us, length us, event | category | flops | bytes accessed | tf_op | source)
XLA Modules:
  0.0 285.5 jit_solution(13614179883614619765)
XLA Ops:
  11.1 15.5 %all-to-all-start.1 = ((bf16[32,1,8,2048]{3,2,1,0:T(8,128)(2,1)}), bf16[32,1,8,2048]{3,2,1,0:T(8,128)(2,1)S(1)}, u32[]{:S(2)}, u32[]{:S(2)}) async-start(bf16[32,1,8,2048]{3,2,1,0:T(8,128)(2,1)} %fusion.5), calls=%async_computation.1 | async-start | bytes 2097152 | tf_op jit(solution)/shard_map/all_to_all | solution.py:52
  28.0 54.5 %all-to-all-done.1 = bf16[32,1,8,2048]{3,2,1,0:T(8,128)(2,1)S(1)} async-done(((bf16[32,1,8,2048]{3,2,1,0:T(8,128)(2,1)}), bf16[32,1,8,2048]{3,2,1,0:T(8,128)(2,1)S(1)}, u32[]{:S(2)}, u32[]{:S(2)}) %all-to-all-start.1) | async-done | bytes 1048608 | tf_op jit(solution)/shard_map/all_to_all | solution.py:52
  82.6 4.7 %all-to-all-start = ((bf16[32,1,8,2048]{3,2,1,0:T(8,128)(2,1)}), bf16[32,1,8,2048]{3,2,1,0:T(8,128)(2,1)}, u32[]{:S(2)}, u32[]{:S(2)}) async-start(bf16[32,1,8,2048]{3,2,1,0:T(8,128)(2,1)} %fusion.4), calls=%async_computation | async-start | bytes 2097152 | tf_op jit(solution)/shard_map/all_to_all | solution.py:53
  88.0 3.5 %collective-permute-start = (bf16[1,512,352]{1,2,0:T(8,128)(2,1)S(1)}, bf16[1,512,352]{1,2,0:T(8,128)(2,1)S(1)}, u32[]{:S(2)}, u32[]{:S(2)}) collective-permute-start(bf16[1,512,352]{1,2,0:T(8,128)(2,1)S(1)} %copy-done.2), channel_id=1, source_target_pairs={{0,128},{128,256},{256,384},{384,0},{1,129},{129,257},{257,385},{3... | collective-permute-start | bytes 1081352 | tf_op jit(solution)/shard_map/ppermute | solution.py:34
  91.6 8.7 %collective-permute-done = bf16[1,512,352]{1,2,0:T(8,128)(2,1)S(1)} collective-permute-done((bf16[1,512,352]{1,2,0:T(8,128)(2,1)S(1)}, bf16[1,512,352]{1,2,0:T(8,128)(2,1)S(1)}, u32[]{:S(2)}, u32[]{:S(2)}) %collective-permute-start) | collective-permute-done | bytes 360480 | tf_op jit(solution)/shard_map/ppermute | solution.py:34
  100.3 3.5 %collective-permute-start.1 = (bf16[1,512,352]{1,2,0:T(8,128)(2,1)S(1)}, bf16[1,512,352]{1,2,0:T(8,128)(2,1)S(1)}, u32[]{:S(2)}, u32[]{:S(2)}) collective-permute-start(bf16[1,512,352]{1,2,0:T(8,128)(2,1)S(1)} %collective-permute-done), channel_id=1, source_target_pairs={{0,128},{128,256},{256,384},{384,0},{1,129},{129,257},{257,385},{3... | collective-permute-start | bytes 1081352 | tf_op jit(solution)/shard_map/ppermute | solution.py:34
  103.8 2.5 collective-permute-start.2
  106.4 8.3 %collective-permute-done.1 = bf16[1,512,352]{1,2,0:T(8,128)(2,1)S(1)} collective-permute-done((bf16[1,512,352]{1,2,0:T(8,128)(2,1)S(1)}, bf16[1,512,352]{1,2,0:T(8,128)(2,1)S(1)}, u32[]{:S(2)}, u32[]{:S(2)}) %collective-permute-start.1) | collective-permute-done | bytes 360480 | tf_op jit(solution)/shard_map/ppermute | solution.py:34
  117.2 3.5 %collective-permute-done.2 = bf16[1,512,352]{1,2,0:T(8,128)(2,1)S(1)} collective-permute-done((bf16[1,512,352]{1,2,0:T(8,128)(2,1)S(1)}, bf16[1,512,352]{1,2,0:T(8,128)(2,1)S(1)}, u32[]{:S(2)}, u32[]{:S(2)}) %collective-permute-start.2) | collective-permute-done | bytes 360480 | tf_op jit(solution)/shard_map/ppermute | solution.py:36
  124.7 2.6 all-gather.5.cloned.1.call-done
  127.3 1.9 fusion.8
  129.3 14.5 %all-to-all-done = bf16[32,1,8,2048]{3,2,1,0:T(8,128)(2,1)} async-done(((bf16[32,1,8,2048]{3,2,1,0:T(8,128)(2,1)}), bf16[32,1,8,2048]{3,2,1,0:T(8,128)(2,1)}, u32[]{:S(2)}, u32[]{:S(2)}) %all-to-all-start) | async-done | bytes 1048608 | tf_op jit(solution)/shard_map/all_to_all | solution.py:53
  143.7 2.3 multiply_convert_fusion
  146.0 17.8 %all-gather.3.cloned.1.call-done = bf16[1,2048,352]{1,2,0:T(8,128)(2,1)} async-done(((bf16[1,512,352]{1,2,0:T(8,128)(2,1)}), bf16[1,2048,352]{1,2,0:T(8,128)(2,1)}) %all-gather.3.cloned.1.call-update) | async-done | bytes 1441808 | tf_op jit(solution)/shard_map/all_gather | solution.py:43
  163.7 1.9 fusion.25
  165.7 1.7 fusion.1
  169.5 2.9 %copy.21 = bf16[1,1,256,2048]{3,1,0,2:T(2,128)(2,1)} copy(bf16[1,1,256,2048]{3,2,1,0:T(8,128)(2,1)S(1)} %fusion.3) | data formatting | bytes 2097152 | tf_op jit(solution)/shard_map/reshape | solution.py:84
  173.0 8.0 %reduce = bf16[256,2048]{1,0:T(8,128)(2,1)S(1)} reduce(bf16[256,1,1,2048]{3,2,1,0:T(2,128)(2,1)} %bitcast.66, bf16[]{:T(256)} %broadcast.20), dimensions={1,2}, to_apply=%bitcast.65.reduce_sub_computation | reduce | bytes 2097154
  181.0 1.9 reshape.108
  182.9 12.6 %all-to-all-start.2 = ((bf16[32,2,8192]{2,1,0:T(2,128)(2,1)}), bf16[32,2,8192]{2,1,0:T(2,128)(2,1)S(1)}, u32[]{:S(2)}, u32[]{:S(2)}) async-start(bf16[32,2,8192]{2,1,0:T(2,128)(2,1)} %reshape.108), calls=%async_computation.2 | async-start | bytes 2097152 | tf_op jit(solution)/shard_map/all_to_all | solution.py:87
  197.3 54.2 %all-to-all-done.2 = bf16[32,2,8192]{2,1,0:T(2,128)(2,1)S(1)} async-done(((bf16[32,2,8192]{2,1,0:T(2,128)(2,1)}), bf16[32,2,8192]{2,1,0:T(2,128)(2,1)S(1)}, u32[]{:S(2)}, u32[]{:S(2)}) %all-to-all-start.2) | async-done | bytes 1048608 | tf_op jit(solution)/shard_map/all_to_all | solution.py:87
  251.5 3.5 %reshape.109 = bf16[256,1,1,2048]{3,2,1,0:T(2,128)(2,1)} reshape(bf16[32,2,8192]{2,1,0:T(2,128)(2,1)S(1)} %all-to-all-done.2) | data formatting | bytes 2097152
  255.0 3.1 %convolution_convert_fusion.4 = bf16[128,2048]{1,0:T(8,128)(2,1)} fusion(bf16[1,1,256,2048]{3,1,0,2:T(2,128)(2,1)} %bitcast.67, s32[128]{0:T(128)S(1)} %multiply_add_fusion), kind=kOutput, calls=%fused_computation.11 | convolution fusion | flops 134512640 | bytes 1573376 | tf_op jit(solution)/shard_map/dot_general | solution.py:89
  258.2 20.8 %reduce-scatter.4.cloned.1.call-done = bf16[128,512]{1,0:T(8,128)(2,1)} async-done(((bf16[128,2048]{1,0:T(8,128)(2,1)}), bf16[128,512]{1,0:T(8,128)(2,1)}) %reduce-scatter.4.cloned.1.call-update) | async-done | bytes 131088 | tf_op jit(solution)/shard_map/reduce_scatter | solution.py:90
  (40 shorter events, 17.1 us)
Async XLA Ops:
  7.2 2.5 copy-start
  7.2 19.4 %copy-start.4 = (bf16[128,2048]{1,0:T(8,128)(2,1)S(1)}, bf16[128,2048]{1,0:T(8,128)(2,1)}, u32[]{:S(2)}) copy-start(bf16[128,2048]{1,0:T(8,128)(2,1)} %param.7) | copy-start | bytes 1572868
  11.1 71.5 %all-to-all-start.1 = ((bf16[32,1,8,2048]{3,2,1,0:T(8,128)(2,1)}), bf16[32,1,8,2048]{3,2,1,0:T(8,128)(2,1)S(1)}, u32[]{:S(2)}, u32[]{:S(2)}) async-start(bf16[32,1,8,2048]{3,2,1,0:T(8,128)(2,1)} %fusion.5), calls=%async_computation.1 | async-start | bytes 2097152 | tf_op jit(solution)/shard_map/all_to_all | solution.py:52
  26.6 61.4 %copy-start.2 = (bf16[1,512,352]{1,2,0:T(8,128)(2,1)S(1)}, bf16[1,512,352]{1,2,0:T(8,128)(2,1)}, u32[]{:S(2)}) copy-start(bf16[1,512,352]{1,2,0:T(8,128)(2,1)} %param.11) | copy-start | bytes 1081348
  82.6 61.2 %all-to-all-start = ((bf16[32,1,8,2048]{3,2,1,0:T(8,128)(2,1)}), bf16[32,1,8,2048]{3,2,1,0:T(8,128)(2,1)}, u32[]{:S(2)}, u32[]{:S(2)}) async-start(bf16[32,1,8,2048]{3,2,1,0:T(8,128)(2,1)} %fusion.4), calls=%async_computation | async-start | bytes 2097152 | tf_op jit(solution)/shard_map/all_to_all | solution.py:53
  87.2 40.1 %all-gather.5.cloned.1.call-start = ((), (), s32[]{:S(2)}) async-start(), calls=%async_computation.7 | async-start | bytes 1802240 | tf_op jit(solution)/shard_map/all_gather | solution.py:42
  88.0 75.8 %all-gather.3.cloned.1.call-start = ((), (), s32[]{:S(2)}) async-start(), calls=%async_computation.6 | async-start | bytes 1802240 | tf_op jit(solution)/shard_map/all_gather | solution.py:43
  88.0 12.3 %collective-permute-start = (bf16[1,512,352]{1,2,0:T(8,128)(2,1)S(1)}, bf16[1,512,352]{1,2,0:T(8,128)(2,1)S(1)}, u32[]{:S(2)}, u32[]{:S(2)}) collective-permute-start(bf16[1,512,352]{1,2,0:T(8,128)(2,1)S(1)} %copy-done.2), channel_id=1, source_target_pairs={{0,128},{128,256},{256,384},{384,0},{1,129},{129,257},{257,385},{3... | collective-permute-start | bytes 1081352 | tf_op jit(solution)/shard_map/ppermute | solution.py:34
  91.6 166.6 %reduce-scatter.6.cloned.1.call-start = ((), (), s32[]{:S(2)}) async-start(), calls=%async_computation.9 | async-start | bytes 1802240 | tf_op jit(solution)/shard_map/reduce_scatter | solution.py:76
  100.3 14.4 %collective-permute-start.1 = (bf16[1,512,352]{1,2,0:T(8,128)(2,1)S(1)}, bf16[1,512,352]{1,2,0:T(8,128)(2,1)S(1)}, u32[]{:S(2)}, u32[]{:S(2)}) collective-permute-start(bf16[1,512,352]{1,2,0:T(8,128)(2,1)S(1)} %collective-permute-done), channel_id=1, source_target_pairs={{0,128},{128,256},{256,384},{384,0},{1,129},{129,257},{257,385},{3... | collective-permute-start | bytes 1081352 | tf_op jit(solution)/shard_map/ppermute | solution.py:34
  103.8 16.9 %collective-permute-start.2 = (bf16[1,512,352]{1,2,0:T(8,128)(2,1)S(1)}, bf16[1,512,352]{1,2,0:T(8,128)(2,1)S(1)}, u32[]{:S(2)}, u32[]{:S(2)}) collective-permute-start(bf16[1,512,352]{1,2,0:T(8,128)(2,1)S(1)} %copy-done.2), channel_id=1, source_target_pairs={{0,384},{128,0},{256,128},{384,256},{1,385},{129,1},{257,129},{385... | collective-permute-start | bytes 1081352 | tf_op jit(solution)/shard_map/ppermute | solution.py:36
  165.7 1.7 copy-start.1
  167.4 1.4 copy-start.3
  182.9 68.6 %all-to-all-start.2 = ((bf16[32,2,8192]{2,1,0:T(2,128)(2,1)}), bf16[32,2,8192]{2,1,0:T(2,128)(2,1)S(1)}, u32[]{:S(2)}, u32[]{:S(2)}) async-start(bf16[32,2,8192]{2,1,0:T(2,128)(2,1)} %reshape.108), calls=%async_computation.2 | async-start | bytes 2097152 | tf_op jit(solution)/shard_map/all_to_all | solution.py:87
  195.5 62.7 %reduce-scatter.8.cloned.1.call-start = ((), (), s32[]{:S(2)}) async-start(), calls=%async_computation.10 | async-start | bytes 1802240 | tf_op jit(solution)/shard_map/reduce_scatter | solution.py:79
  197.2 81.7 %reduce-scatter.4.cloned.1.call-start = ((), (), s32[]{:S(2)}) async-start(), calls=%async_computation.8 | async-start | bytes 655360 | tf_op jit(solution)/shard_map/reduce_scatter | solution.py:90
Sparse Core Ops, SparseCore 0:
  90.2 37.0 all-gather.4
  129.4 34.2 all-gather.2
  167.5 32.7 reduce-scatter.5
  203.6 32.5 reduce-scatter.7
  258.3 20.6 reduce-scatter.3
